TPU v7x, 32 devices: a whole 2x2x4 slice. The times are simulated.
32 devices in a mesh: fsdp: 32 (over z, y, x, core).
Axes of the slice: x: 2, y: 2, z: 4, core: 2. Of those that a mesh axis runs over, the one named last changes fastest.
Arguments:
- tokens: bfloat16 [4096, 1024], P('fsdp'), may hold values from -160 to 160
- seq_ids: int32 [4096], P('fsdp'), may hold values from 0 to 64, as said below
- grad_output: bfloat16 [4096, 1024], P('fsdp'), may hold values from -6 to 6
- qkv_weight: bfloat16 [3145728], P('fsdp'), may hold values from -0.1875 to 0.1875
- out_weight: bfloat16 [1048576], P('fsdp'), may hold values from -1 to 1
- up_weight: bfloat16 [4194304], P('fsdp'), may hold values from -0.1875 to 0.1875
- down_weight: bfloat16 [4194304], P('fsdp'), may hold values from -0.09375 to 0.09375
- small_params: bfloat16 [12288], P('fsdp'), may hold values from 0.5 to 1.5
Outputs:
- output: bfloat16 [4096, 1024], P('fsdp')
- tokens_grad: bfloat16 [4096, 1024], P('fsdp')
- qkv_weight_grad: float32 [3145728], P('fsdp')
- out_weight_grad: float32 [1048576], P('fsdp')
- up_weight_grad: float32 [4194304], P('fsdp')
- down_weight_grad: float32 [4194304], P('fsdp')
- small_params_grad: float32 [12288], P('fsdp')
Inputs may be any that keep to these rules, and one draw needn't show every extreme that they name: `seq_ids`: within each block of 128 rows the numbers start at 0, rise by one at the first row of each new sequence and never fall; a sequence holds 1 to 64 rows, never crosses a multiple of 64 rows, and every block holds one sequence of exactly 64 rows.
All inputs are finite; a program needn't handle non-finite values.
Results may differ from a plain program's by a relative error of at most 0.012.
The roundings to bfloat16 on the way count: a program that leaves them out, or rounds other values in their place, can miss the bound.
Values may be sent and summed in bfloat16 or wider, within the bound.
A program may use at most 256 MiB of HBM per device.

v0:
```python
import functools

import jax
import jax.numpy as jnp
from jax import lax
from jax.experimental import pallas as pl
from jax.experimental.pallas import tpu as pltpu
from jax.sharding import PartitionSpec as P

D = 1024
HEAD_DIM = 64
FF = 4096
TOK_DEV = 128


EPS = 1e-06
ROOT_HALF = 0.7071067811865476
INV_ROOT_TAU = 0.3989422804014327


def matmul(former, latter):
    return jnp.dot(former, latter, preferred_element_type=jnp.float32)


def matmul_tn(former, latter):
    return lax.dot_general(
        former, latter, (((0,), (0,)), ((), ())), preferred_element_type=jnp.float32
    )


def matmul_nt(former, latter):
    return lax.dot_general(
        former, latter, (((1,), (1,)), ((), ())), preferred_element_type=jnp.float32
    )


def unpack(params):
    params = params.astype(jnp.float32)
    bounds = [0, D, 2 * D, 3 * D, 4 * D, 5 * D, 5 * D + FF, 6 * D + FF, 7 * D + FF, 8 * D + FF]
    return [params[bounds[position] : bounds[position + 1]] for position in range(9)]


def norm_forward(values, gain, shift):
    center = values - jnp.mean(values, axis=-1, keepdims=True)
    inverse = lax.rsqrt(jnp.mean(center * center, axis=-1, keepdims=True) + EPS)
    normed = center * inverse
    return (normed * gain + shift, normed, inverse)


def norm_backward(upstream, normed, inverse, gain):
    scaled = upstream * gain
    return inverse * (
        scaled
        - jnp.mean(scaled, axis=-1, keepdims=True)
        - normed * jnp.mean(scaled * normed, axis=-1, keepdims=True)
    )


def gelu_curve(values):
    return 0.5 * values * (1.0 + lax.erf(values * ROOT_HALF))


def gelu_slope(values):
    return (
        0.5 * (1.0 + lax.erf(values * ROOT_HALF))
        + values * jnp.exp(-0.5 * values * values) * INV_ROOT_TAU
    )


def split_heads(matrix):
    return matrix.reshape(-1, TOK_DEV, matrix.shape[1] // HEAD_DIM, HEAD_DIM)


def block_mask(ids):
    blocks = ids.reshape(-1, TOK_DEV)
    return (blocks[:, :, None] == blocks[:, None, :])[:, None]


def masked_scores(queries, key_rows, same_seq):
    scores = jnp.einsum(
        "bqhd,bkhd->bhqk",
        split_heads(queries),
        split_heads(key_rows),
        preferred_element_type=jnp.float32,
    ) * HEAD_DIM ** (-0.5)
    return jnp.where(same_seq, scores, -jnp.inf)


def attend(queries, key_rows, value_rows, same_seq):
    scores = masked_scores(queries, key_rows, same_seq)
    row_max = jnp.max(scores, axis=-1, keepdims=True)
    log_total = row_max + jnp.log(jnp.sum(jnp.exp(scores - row_max), axis=-1, keepdims=True))
    attn_probs = jnp.exp(scores - log_total).astype(jnp.bfloat16)
    context = (
        jnp.einsum(
            "bhqk,bkhd->bqhd",
            attn_probs,
            split_heads(value_rows),
            preferred_element_type=jnp.float32,
        )
        .reshape(-1, queries.shape[1])
        .astype(jnp.bfloat16)
    )
    return (context, log_total)


def attend_back(queries, key_rows, value_rows, same_seq, log_total, context_grad):
    columns = queries.shape[1]
    probs_full = jnp.exp(masked_scores(queries, key_rows, same_seq) - log_total)
    probs_bf = probs_full.astype(jnp.bfloat16)
    prob_grad = jnp.einsum(
        "bqhd,bkhd->bhqk",
        split_heads(context_grad),
        split_heads(value_rows),
        preferred_element_type=jnp.float32,
    )
    value_grad = jnp.einsum(
        "bhqk,bqhd->bkhd", probs_bf, split_heads(context_grad), preferred_element_type=jnp.float32
    ).reshape(-1, columns)
    row_delta = jnp.sum(probs_full * prob_grad, axis=-1, keepdims=True)
    score_grad = (probs_full * (prob_grad - row_delta) * HEAD_DIM ** (-0.5)).astype(jnp.bfloat16)
    query_grad = jnp.einsum(
        "bhqk,bkhd->bqhd", score_grad, split_heads(key_rows), preferred_element_type=jnp.float32
    ).reshape(-1, columns)
    key_grad = jnp.einsum(
        "bhqk,bqhd->bkhd", score_grad, split_heads(queries), preferred_element_type=jnp.float32
    ).reshape(-1, columns)
    return (query_grad, key_grad, value_grad)


def forward_pass(tokens, seq_ids, weights):
    qkv_matrix, out_matrix, up_matrix, down_matrix, bias_gain = weights
    (
        query_bias,
        value_bias,
        out_bias,
        gain_one,
        shift_one,
        up_bias,
        down_bias,
        gain_two,
        shift_two,
    ) = unpack(bias_gain)
    same_seq = block_mask(seq_ids)
    projected = matmul(tokens, qkv_matrix)
    queries = (projected[:, :D] + query_bias).astype(jnp.bfloat16)
    key_rows = projected[:, D : 2 * D].astype(jnp.bfloat16)
    value_rows = (projected[:, 2 * D :] + value_bias).astype(jnp.bfloat16)
    context, log_total = attend(queries, key_rows, value_rows, same_seq)
    first_sum = tokens.astype(jnp.float32) + matmul(context, out_matrix) + out_bias
    first_norm, first_unit, first_inv = norm_forward(first_sum, gain_one, shift_one)
    first_bf = first_norm.astype(jnp.bfloat16)
    hidden_pre = matmul(first_bf, up_matrix) + up_bias
    activated = gelu_curve(hidden_pre).astype(jnp.bfloat16)
    second_sum = first_norm + matmul(activated, down_matrix) + down_bias
    result, second_unit, second_inv = norm_forward(second_sum, gain_two, shift_two)
    kept = (
        same_seq,
        queries,
        key_rows,
        value_rows,
        log_total,
        context,
        first_unit,
        first_inv,
        first_bf,
        hidden_pre,
        activated,
        second_unit,
        second_inv,
    )
    return (result.astype(jnp.bfloat16), kept)


def mlp_backward(grad_output, kept, weights):
    qkv_matrix, out_matrix, up_matrix, down_matrix, bias_gain = weights
    gain_two = unpack(bias_gain)[7]
    first_bf, hidden_pre, activated, second_unit, second_inv = (
        kept[8],
        kept[9],
        kept[10],
        kept[11],
        kept[12],
    )
    out_cot = grad_output.astype(jnp.float32)
    gain_two_grad = jnp.sum(out_cot * second_unit, axis=0)
    shift_two_grad = jnp.sum(out_cot, axis=0)
    second_grad = norm_backward(out_cot, second_unit, second_inv, gain_two)
    down_bias_grad = jnp.sum(second_grad, axis=0)
    second_bf = second_grad.astype(jnp.bfloat16)
    down_grad = matmul_tn(activated, second_bf)
    hidden_grad = matmul_nt(second_bf, down_matrix) * gelu_slope(hidden_pre)
    up_bias_grad = jnp.sum(hidden_grad, axis=0)
    hidden_bf = hidden_grad.astype(jnp.bfloat16)
    up_grad = matmul_tn(first_bf, hidden_bf)
    first_grad = second_grad + matmul_nt(hidden_bf, up_matrix)
    return (
        first_grad,
        up_grad,
        down_grad,
        (up_bias_grad, down_bias_grad, gain_two_grad, shift_two_grad),
    )


def attention_backward(tokens, first_grad, kept, weights):
    qkv_matrix, out_matrix, up_matrix, down_matrix, bias_gain = weights
    gain_one = unpack(bias_gain)[3]
    same_seq, queries, key_rows, value_rows, log_total, context, first_unit, first_inv = kept[:8]
    gain_one_grad = jnp.sum(first_grad * first_unit, axis=0)
    shift_one_grad = jnp.sum(first_grad, axis=0)
    residual_grad = norm_backward(first_grad, first_unit, first_inv, gain_one)
    out_bias_grad = jnp.sum(residual_grad, axis=0)
    residual_bf = residual_grad.astype(jnp.bfloat16)
    out_grad = matmul_tn(context, residual_bf)
    context_grad = matmul_nt(residual_bf, out_matrix).astype(jnp.bfloat16)
    query_grad, key_grad, value_grad = attend_back(
        queries, key_rows, value_rows, same_seq, log_total, context_grad
    )
    query_bias_grad = jnp.sum(query_grad, axis=0)
    value_bias_grad = jnp.sum(value_grad, axis=0)
    joined_bf = jnp.concatenate([query_grad, key_grad, value_grad], axis=1).astype(jnp.bfloat16)
    qkv_grad = matmul_tn(tokens, joined_bf)
    tokens_grad = (residual_grad + matmul_nt(joined_bf, qkv_matrix)).astype(jnp.bfloat16)
    return (
        tokens_grad,
        qkv_grad,
        out_grad,
        (query_bias_grad, value_bias_grad, out_bias_grad, gain_one_grad, shift_one_grad),
    )


def bit_orders(count):
    bits = count.bit_length() - 1
    first = list(range(bits))
    second, third, fourth = list(first), list(first), list(first)
    if bits > 2:
        second[1], second[2] = 2, 1
    if bits > 3:
        third[1:4] = [3, 1, 2]
        fourth[1:4] = [3, 2, 1]
    return first, second, third, fourth


def column_pieces(widths, parts, orders):
    first, second, third, fourth = orders
    cycle = (first, second, third, first, second, fourth)
    plans = []
    for array, (width, count) in enumerate(zip(widths, parts)):
        size = width // count
        for part in range(count):
            plans.append((array, part * size, size, cycle[len(plans) % len(cycle)]))
    return tuple(plans)


def wavefront(pieces, steps):
    pairs = [(piece, step) for piece in range(pieces) for step in range(steps)]
    return sorted(pairs, key=lambda pair: (pair[0] + 2 * pair[1], -pair[1]))


def row_blocks(matrix):
    count = lax.axis_size("fsdp")
    rows, columns = matrix.shape[0] // count, matrix.shape[1]
    folds = max(1, 16 // rows)
    return matrix.reshape(count, rows * folds, columns // folds)


def scatter_kernel(count, plans, arrays, *refs):
    bits = count.bit_length() - 1
    ins, outs = refs[:arrays], refs[arrays : 2 * arrays]
    held = refs[2 * arrays : 2 * arrays + arrays * bits]
    send_sem, recv_sem = refs[2 * arrays + arrays * bits :]
    me = lax.axis_index("fsdp")

    def side(bit):
        return (me // 2**bit) % 2

    def partner(bit):
        return me + 2**bit * (1 - 2 * side(bit))

    barrier = pltpu.get_barrier_semaphore()
    for bit in range(bits):
        pl.semaphore_signal(
            barrier, inc=1, device_id=(partner(bit),), device_id_type=pl.DeviceIdType.MESH
        )
    pl.semaphore_wait(barrier, bits)

    def remote(piece, step, source, target):
        return pltpu.make_async_remote_copy(
            src_ref=source,
            dst_ref=target,
            send_sem=send_sem.at[piece, step],
            recv_sem=recv_sem.at[piece, step],
            device_id=(partner(plans[piece][3][step]),),
            device_id_type=pl.DeviceIdType.MESH,
        )

    def whole(piece, step):
        array, start, size, _ = plans[piece]
        block = held[array * bits + step].at[:, :, pl.ds(start, size)]
        return remote(piece, step, block, block)

    def spot(piece, step, turn, half):
        order = plans[piece][3]
        if step > 0:
            return 2 * turn + half
        row = half * 2 ** order[0]
        for position, bit in enumerate(order[1:]):
            row = row + ((turn // 2**position) % 2) * 2**bit
        return row

    def source_of(piece, step):
        array = plans[piece][0]
        return ins[array] if step == 0 else held[array * bits + step - 1]

    def begin(piece, step):
        array, start, size, order = plans[piece]
        columns = pl.ds(start, size)
        other = 1 - side(order[step])

        def send(turn, carry):
            remote(
                piece,
                step,
                source_of(piece, step).at[spot(piece, step, turn, other), :, columns],
                held[array * bits + step].at[turn, :, columns],
            ).start()
            return carry

        lax.fori_loop(0, count // 2 ** (step + 1), send, 0)

    def add(piece, step):
        array, start, size, order = plans[piece]
        columns = pl.ds(start, size)
        mine = side(order[step])
        target = held[array * bits + step]

        def one(turn, carry):
            kept = source_of(piece, step)[spot(piece, step, turn, mine), :, columns]
            total = kept.astype(jnp.float32) + target[turn, :, columns].astype(jnp.float32)
            if step == bits - 1:
                outs[array][:, columns] = total
            else:
                target[turn, :, columns] = total.astype(target.dtype)
            return carry

        lax.fori_loop(0, count // 2 ** (step + 1), one, 0)

    for piece in range(len(plans)):
        begin(piece, 0)
    for piece, step in wavefront(len(plans), bits):
        whole(piece, step).wait_recv()
        add(piece, step)
        if step + 1 < bits:
            begin(piece, step + 1)
    for piece in range(len(plans)):
        for step in range(bits):
            whole(piece, step).wait_send()


def scatter_all(blocks):
    count = lax.axis_size("fsdp")
    bits = count.bit_length() - 1
    plans = column_pieces(
        [block.shape[2] for block in blocks], (4, 4, 3, 1, 1), bit_orders(count)
    )
    return pl.pallas_call(
        functools.partial(scatter_kernel, count, plans, len(blocks)),
        out_shape=[jax.ShapeDtypeStruct(block.shape[1:], jnp.float32) for block in blocks],
        in_specs=[pl.BlockSpec(memory_space=pltpu.VMEM)] * len(blocks),
        out_specs=[pl.BlockSpec(memory_space=pltpu.VMEM)] * len(blocks),
        scratch_shapes=[
            pltpu.VMEM((count // 2 ** (step + 1),) + block.shape[1:], block.dtype)
            for block in blocks
            for step in range(bits)
        ]
        + [
            pltpu.SemaphoreType.DMA((len(plans), bits)),
            pltpu.SemaphoreType.DMA((len(plans), bits)),
        ],
        compiler_params=pltpu.CompilerParams(
            collective_id=1, has_side_effects=True, vmem_limit_bytes=64000000
        ),
    )(*blocks)


def gather_kernel(count, plans, arrays, *refs):
    ins, outs = refs[:arrays], refs[arrays : 2 * arrays]
    local_sem, send_sem, recv_sem = refs[2 * arrays :]
    me = lax.axis_index("fsdp")
    bits = count.bit_length() - 1

    def partner(bit):
        return me + 2**bit * (1 - 2 * ((me // 2**bit) % 2))

    barrier = pltpu.get_barrier_semaphore()
    for bit in range(bits):
        pl.semaphore_signal(
            barrier, inc=1, device_id=(partner(bit),), device_id_type=pl.DeviceIdType.MESH
        )
    pl.semaphore_wait(barrier, bits)

    def own_copy(piece):
        array, start, size, _ = plans[piece]
        columns = pl.ds(start, size)
        return pltpu.make_async_copy(
            ins[array].at[:, columns], outs[array].at[me, :, columns], local_sem.at[piece]
        )

    def remote(piece, step, source, target):
        return pltpu.make_async_remote_copy(
            src_ref=source,
            dst_ref=target,
            send_sem=send_sem.at[piece, step],
            recv_sem=recv_sem.at[piece, step],
            device_id=(partner(plans[piece][3][step]),),
            device_id_type=pl.DeviceIdType.MESH,
        )

    def whole(piece, step):
        array, start, size, _ = plans[piece]
        block = outs[array].at[pl.ds(0, 2**step), :, pl.ds(start, size)]
        return remote(piece, step, block, block)

    def begin(piece, step):
        array, start, size, order = plans[piece]
        columns = pl.ds(start, size)
        if step == 0:
            remote(
                piece, step, ins[array].at[:, columns], outs[array].at[me, :, columns]
            ).start()
            return
        base = me
        for bit in order[:step]:
            base = base - ((me // 2**bit) % 2) * 2**bit

        def send(turn, carry):
            row = base
            for position, bit in enumerate(order[:step]):
                row = row + ((turn // 2**position) % 2) * 2**bit
            block = outs[array].at[row, :, columns]
            remote(piece, step, block, block).start()
            return carry

        lax.fori_loop(0, 2**step, send, 0)

    pieces = range(len(plans))
    for piece in pieces:
        begin(piece, 0)
    for piece in pieces:
        own_copy(piece).start()
    for piece, step in wavefront(len(plans), bits):
        whole(piece, step).wait_recv()
        if step == 0:
            own_copy(piece).wait()
        if step + 1 < bits:
            begin(piece, step + 1)
    for step in range(bits):
        for piece in pieces:
            whole(piece, step).wait_send()


def gather_all(blocks):
    count = lax.axis_size("fsdp")
    plans = column_pieces(
        [block.shape[1] for block in blocks],
        (3, 1, 4, 4, 1),
        [order[::-1] for order in bit_orders(count)],
    )
    bits = count.bit_length() - 1
    results = pl.pallas_call(
        functools.partial(gather_kernel, count, plans, len(blocks)),
        out_shape=[jax.ShapeDtypeStruct((count,) + block.shape, block.dtype) for block in blocks],
        in_specs=[pl.BlockSpec(memory_space=pltpu.VMEM)] * len(blocks),
        out_specs=[pl.BlockSpec(memory_space=pl.ANY)] * len(blocks),
        scratch_shapes=[
            pltpu.SemaphoreType.DMA((len(plans),)),
            pltpu.SemaphoreType.DMA((len(plans), bits)),
            pltpu.SemaphoreType.DMA((len(plans), bits)),
        ],
        compiler_params=pltpu.CompilerParams(collective_id=0, has_side_effects=True),
    )(*blocks)
    return tuple(result.reshape(-1, result.shape[2]) for result in results[:4]) + (
        results[4].reshape(-1),
    )


def shards(
    tokens, seq_ids, grad_output, qkv_weight, out_weight, up_weight, down_weight, small_params
):
    weights = gather_all(
        (
            qkv_weight.reshape(-1, 3 * D),
            out_weight.reshape(-1, D),
            up_weight.reshape(-1, FF),
            down_weight.reshape(-1, D),
            small_params.reshape(1, -1),
        )
    )
    result, kept = forward_pass(tokens, seq_ids, weights)
    first_grad, up_grad, down_grad, mlp_small = mlp_backward(grad_output, kept, weights)
    tokens_grad, qkv_grad, out_grad, attn_small = attention_backward(
        tokens, first_grad, kept, weights
    )
    small_grad = jnp.concatenate(list(attn_small) + list(mlp_small))
    down_share, up_share, qkv_share, out_share, small_share = scatter_all(
        [row_blocks(grad.astype(jnp.bfloat16)) for grad in (down_grad, up_grad, qkv_grad, out_grad)]
        + [small_grad.reshape(lax.axis_size("fsdp"), 1, -1)]
    )
    return (
        result,
        tokens_grad,
        qkv_share.reshape(-1),
        out_share.reshape(-1),
        up_share.reshape(-1),
        down_share.reshape(-1),
        small_share.reshape(-1),
    )


def solution(mesh):
    in_specs = (
        P("fsdp", None),
        P("fsdp"),
        P("fsdp", None),
        P("fsdp"),
        P("fsdp"),
        P("fsdp"),
        P("fsdp"),
        P("fsdp"),
    )
    out_specs = (
        P("fsdp", None),
        P("fsdp", None),
        P("fsdp"),
        P("fsdp"),
        P("fsdp"),
        P("fsdp"),
        P("fsdp"),
    )
    return jax.shard_map(shards, mesh=mesh, in_specs=in_specs, out_specs=out_specs, check_vma=False)
```

profile of v0, /device:TPU:0, one launch (start us, length us, event | category | flops | bytes accessed | tf_op | source)
XLA Modules:
  0.0 340.5 jit_solution(1381454449436264782)
XLA Ops:
  0.6 1.3 reshape.271.refs_4_
  1.9 0.8 broadcast_compare_fusion
  2.7 1.5 reshape.268.refs_1_
  4.3 1.7 reshape.267.refs_0_
  5.9 1.8 reshape.269.refs_2_
  7.7 1.8 reshape.270.refs_3_
  9.5 130.8 %shard_map.135 = (bf16[32,32,3072]{2,1,0:T(8,128)(2,1)}, bf16[32,32,1024]{2,1,0:T(8,128)(2,1)}, bf16[32,32,4096]{2,1,0:T(8,128)(2,1)}, bf16[32,128,1024]{2,1,0:T(8,128)(2,1)}, bf16[32,1,384]{2,1,0:T(2,128)(2,1)}) custom-call(bf16[32,3072]{1,0:T(8,128)(2,1)} %reshape.267.refs_0_, bf16[32,1024]{1,0:T(8,128)(2,1)} %reshape.268.refs_1_, ...), custom_call_target="tpu_custom_call" | custom-call | tf_op jit(solution)/shard_map/pallas_call | solution.py:470
  140.3 1.0 convert_element_type.110
  141.3 4.9 %convolution_bitcast_fusion = f32[128,3072]{0,1:T(8,128)S(1)} fusion(bf16[1024,3072]{1,0:T(8,128)(2,1)} %bitcast.79, bf16[128,1024]{1,0:T(8,128)(2,1)S(1)} %copy-done.6), kind=kOutput, calls=%fused_computation.6 | convolution fusion | flops 805306368 | bytes 8126464 | tf_op jit(solution)/shard_map/dot_general | solution.py:22
  146.2 0.3 fusion.26
  146.6 0.4 fusion.57
  147.0 0.2 exponential_reduce_fusion
  147.2 0.1 copy-done.14
  147.3 0.3 convolution_convert_fusion.6
  147.6 1.3 copy-done.1
  148.9 0.5 fusion.58
  149.4 0.2 multiply_reduce_fusion.4
  149.7 1.3 convolution_add_fusion
  151.0 0.6 slice-done.2
  151.6 1.3 slice-done.3
  153.0 1.5 fusion.59
  154.5 0.2 multiply_reduce_fusion.3
  154.7 0.3 fusion.25
  155.0 1.0 fusion.51
  156.0 3.4 %fusion.62 = (f32[4096]{0:T(1024)S(1)}, bf16[128,4096]{1,0:T(8,128)(2,1)S(1)}) fusion(f32[128,4096]{1,0:T(8,128)S(1)} %convolution_add_fusion, bf16[4096,1024]{1,0:T(8,128)(2,1)S(1)} %bitcast.78, f32[128,1024]{1,0:T(8,128)S(1)} %get-tuple-element.36), kind=kOutput, calls=%fused_computation.108 | convolution fusion | flops 1079635968 | bytes 12075008 | tf_op jit(solution)/shard_map/dot_general | solution.py:32
  159.4 3.0 multiply_reduce_fusion.1
  162.5 0.2 fusion.53
  162.7 0.0 copy-start.2
  162.7 1.5 convolution_convert_fusion.5
  164.3 1.1 copy.22
  165.4 2.4 fusion.54
  167.8 0.1 reduce_sum.188
  167.9 2.3 fusion.63
  170.2 3.6 %convolution_convert_fusion.4 = bf16[16,64,128]{2,1,0:T(8,128)(2,1)} fusion(bf16[128,16,64]{0,2,1:T(8,128)(2,1)} %bitcast.95, f32[16,128,128]{1,2,0:T(8,128)} %fusion.63, f32[16,128,128]{1,2,0:T(8,128)} %copy-done, f32[16,128]{1,0:T(8,128)S(1)} %log_add_fusion), kind=kOutput, calls=%fused_computation.30 | convolution fusion | flops 35522688 | bytes 2629632 | tf_op jit(solution)/shard_map/bhqk,bqhd->bkhd/dot_general | solution.py:125
  173.8 3.7 %fusion.55 = (f32[16,64]{1,0:T(8,128)S(1)}, bf16[1,128,16,64]{1,3,2,0:T(8,128)(2,1)}) fusion(bf16[128,16,64]{0,2,1:T(8,128)(2,1)} %bitcast.93, f32[16,128,128]{1,2,0:T(8,128)} %fusion.63, f32[16,128,128]{1,2,0:T(8,128)} %copy-done, f32[16,128]{1,0:T(8,128)S(1)} %log_add_fusion), kind=kOutput, calls=%fused_computation.103 | convolution fusion | flops 35652736 | bytes 2633728 | tf_op jit(solution)/shard_map/bhqk,bkhd->bqhd/dot_general | solution.py:122
  177.5 0.1 reduce_sum.186
  177.5 6.0 %fusion.12 = bf16[128,1024]{1,0:T(8,128)(2,1)} fusion(f32[128,1024]{1,0:T(8,128)} %copy-done.2, bf16[1024,3072]{1,0:T(8,128)(2,1)} %bitcast.80, bf16[128,1024]{0,1:T(8,128)(2,1)S(1)} %bitcast.90, bf16[128,1024]{0,1:T(8,128)(2,1)} %bitcast.102, bf16[128,1024]{0,1:T(8,128)(2,1)} %bitcast.104), kind=kOutput, calls=%fused_computation.29 | convolution fusion | flops 807927808 | bytes 7864320 | tf_op jit(solution)/shard_map/dot_general | solution.py:32
  183.6 0.0 copy-start.18
  183.6 2.0 convolution_convert_fusion.3
  185.7 4.5 %convolution_convert_fusion.2 = bf16[3072,1024]{0,1:T(8,128)(2,1)} fusion(bf16[128,1024]{1,0:T(8,128)(2,1)S(1)} %copy-done.7, bf16[128,1024]{0,1:T(8,128)(2,1)S(1)} %bitcast.91, bf16[128,1024]{0,1:T(8,128)(2,1)S(1)} %bitcast.103, bf16[128,1024]{0,1:T(8,128)(2,1)S(1)} %bitcast.105), kind=kOutput, calls=%fused_computation.3 | convolution fusion | flops 810811392 | bytes 7340032 | tf_op jit(solution)/shard_map/dot_general | solution.py:26
  190.2 4.6 %convolution_convert_fusion.1 = bf16[4096,1024]{1,0:T(8,128)(2,1)} fusion(f32[128,1024]{1,0:T(8,128)S(1)} %get-tuple-element.36, f32[128,4096]{1,0:T(8,128)S(1)} %convolution_add_fusion), kind=kOutput, calls=%fused_computation.2 | convolution fusion | flops 1080688640 | bytes 11010048 | tf_op jit(solution)/shard_map/dot_general | solution.py:26
  194.8 5.7 %convolution_convert_fusion = bf16[1024,4096]{1,0:T(8,128)(2,1)} fusion(bf16[128,4096]{1,0:T(8,128)(2,1)S(1)} %copy-done.5, f32[128,1024]{1,0:T(8,128)S(1)} %get-tuple-element.57, f32[1024]{0:T(1024)S(1)} %get-tuple-element.49, f32[1024]{0:T(1024)S(1)} %get-tuple-element.50, f32[128]{0:T(128)S(1)} %add_rsqrt_fusion.1, f32[128]{0:T(128)S(1)} %broadcast_multiply_fusion.5), kind=kOutput, calls=%fused_computation.1 | convolution fusion | flops 1078591488 | bytes 9970688 | tf_op jit(solution)/shard_map/dot_general | solution.py:26
  200.4 132.5 %shard_map.136 = (f32[128,1024]{1,0:T(8,128)}, f32[32,4096]{1,0:T(8,128)}, f32[32,3072]{1,0:T(8,128)}, f32[32,1024]{1,0:T(8,128)}, f32[1,384]{1,0:T(1,128)}) custom-call(bf16[32,128,1024]{2,1,0:T(8,128)(2,1)} %bitcast.68, bf16[32,32,4096]{2,1,0:T(8,128)(2,1)} %bitcast.74, bf16[32,32,3072]{2,1,0:T(8,128)(2,1)} %bitcast.73, bf16[32,32,1024]{2,1,0:T(8,128)(2,1)} %bitcast.83, ...), custom_call_target="tpu_custom_call" | custom-call | tf_op jit(solution)/shard_map/pallas_call | solution.py:366
  333.0 1.9 copy.30
  334.8 1.6 copy.31
  336.4 1.3 reduce.8
  337.7 1.9 copy.32
  339.6 0.9 copy.33
  (62 shorter events, 0.2 us)
Async XLA Ops:
  0.6 140.7 %copy-start.6 = (bf16[128,1024]{1,0:T(8,128)(2,1)S(1)}, bf16[128,1024]{1,0:T(8,128)(2,1)}, u32[]{:S(2)}) copy-start(bf16[128,1024]{1,0:T(8,128)(2,1)} %param.8) | copy-start | bytes 786436
  140.3 9.4 %slice-start = ((s8[8388608]{0:T(1024)(128)(4,1)}), s8[4194304]{0:T(1024)(128)(4,1)S(1)}, s32[]{:S(2)}) async-start(s8[8388608]{0:T(1024)(128)(4,1)} %bitcast.69), calls=%async_computation | async-start | bytes 8388608
  141.3 8.3 %slice-start.1 = ((s8[8388608]{0:T(1024)(128)(4,1)}), s8[4194304]{0:T(1024)(128)(4,1)S(1)}, s32[]{:S(2)}) async-start(s8[8388608]{0:T(1024)(128)(4,1)} %bitcast.69), calls=%async_computation.1 | async-start | bytes 8388608
  146.2 0.9 copy-start.13
  146.6 0.7 copy-start.14
  146.6 1.0 copy-start.8
  146.6 2.3 copy-start.1
  147.0 2.4 copy-start
  147.6 1.8 copy-start.9
  149.4 2.2 slice-start.2
  149.7 3.3 slice-start.3
  153.0 1.8 copy-start.11
  159.4 3.0 copy-start.4
  162.7 1.5 copy-start.2
  170.2 7.4 %copy-start.12 = (bf16[1,128,16,64]{1,3,2,0:T(8,128)(2,1)S(1)}, bf16[1,128,16,64]{1,3,2,0:T(8,128)(2,1)}, u32[]{:S(2)}) copy-start(bf16[1,128,16,64]{1,3,2,0:T(8,128)(2,1)} %get-tuple-element.43) | copy-start | bytes 786436
  177.5 6.1 %copy-start.3 = (f32[128,1024]{1,0:T(8,128)S(1)}, f32[128,1024]{1,0:T(8,128)}, u32[]{:S(2)}) copy-start(f32[128,1024]{1,0:T(8,128)} %copy-done.2) | copy-start | bytes 1572868
  177.5 6.1 %copy-start.10 = (bf16[16,64,128]{2,1,0:T(8,128)(2,1)S(1)}, bf16[16,64,128]{2,1,0:T(8,128)(2,1)}, u32[]{:S(2)}) copy-start(bf16[16,64,128]{2,1,0:T(8,128)(2,1)} %copy-done.9) | copy-start | bytes 786436
  183.5 2.2 copy-start.7
  183.5 2.2 copy-start.16
  183.5 2.2 copy-start.17
  183.6 6.6 %copy-start.18 = (f32[12288]{0:T(1024)}, f32[12288]{0:T(1024)S(1)}, u32[]{:S(2)}) copy-start(f32[12288]{0:T(1024)S(1)} %constant_dynamic-update-slice_fusion) | copy-start | bytes 147460
  190.2 4.6 %copy-start.5 = (bf16[128,4096]{1,0:T(8,128)(2,1)S(1)}, bf16[128,4096]{1,0:T(8,128)(2,1)}, u32[]{:S(2)}) copy-start(bf16[128,4096]{1,0:T(8,128)(2,1)} %copy-done.4) | copy-start | bytes 3145732
  333.0 6.7 %copy-start.15 = (f32[128,1024]{1,0:T(8,128)S(1)}, f32[128,1024]{1,0:T(8,128)}, u32[]{:S(2)}) copy-start(f32[128,1024]{1,0:T(8,128)} %get-tuple-element.25) | copy-start | bytes 1572868
where the time goes:
time: 341 us
  Pallas kernels  263 us (77%)
  matrix products  51.7 us (15%)
  local copies, waits for them, and re-layouts  19 us (6%)
  other arithmetic  5.47 us (2%)
    pallas_call x1, Pallas kernels, scatter_all(): pl.pallas_call(functools.partial(scatter_kernel, count, plans, len(blocks...  133 us
    pallas_call x1, Pallas kernels, gather_all(): pl.pallas_call(functools.partial(gather_kernel, count, plans, len(blocks)...  131 us
    dot_general x4, matrix products, matmul_tn(): lax.dot_general(former, latter, (((0,), (0,)), ((), ())), preferred_eleme...  16.8 us
    dot_general x4, matrix products, matmul_nt(): lax.dot_general(former, latter, (((1,), (1,)), ((), ())), preferred_eleme...  14 us
    unnamed x58, local copies, waits for them, and re-layouts  9.68 us
    dot_general x4, matrix products, matmul(): return jnp.dot(former, latter, preferred_element_type=jnp.float32)  8.27 us

commit v1 on v0

--- a/solution.py
+++ b/solution.py
@@ -254,7 +254,7 @@
 
 def wavefront(pieces, steps):
     pairs = [(piece, step) for piece in range(pieces) for step in range(steps)]
-    return sorted(pairs, key=lambda pair: (pair[0] + 2 * pair[1], -pair[1]))
+    return sorted(pairs, key=lambda pair: (pair[0] + 3 * pair[1], -pair[1]))
 
 
 def row_blocks(matrix):
@@ -361,7 +361,7 @@
     count = lax.axis_size("fsdp")
     bits = count.bit_length() - 1
     plans = column_pieces(
-        [block.shape[2] for block in blocks], (4, 4, 3, 1, 1), bit_orders(count)
+        [block.shape[2] for block in blocks], (8, 8, 6, 2, 1), bit_orders(count)
     )
     return pl.pallas_call(
         functools.partial(scatter_kernel, count, plans, len(blocks)),
@@ -463,7 +463,7 @@
     count = lax.axis_size("fsdp")
     plans = column_pieces(
         [block.shape[1] for block in blocks],
-        (3, 1, 4, 4, 1),
+        (6, 2, 8, 8, 1),
         [order[::-1] for order in bit_orders(count)],
     )
     bits = count.bit_length() - 1

time: 341 us -> 332 us (0.974)
  Pallas kernels: 263 us -> 254 us
    pallas_call x1, Pallas kernels: 133 us -> 124 us  [scatter_all(): pl.pallas_call(functools.partial(scatter_kernel, count, plans, len(blocks...]
where the time goes in v1:
time: 332 us; the launch traced here: 331 us
  Pallas kernels  254 us (77%)
  matrix products  51.7 us (16%)
  local copies, waits for them, and re-layouts  19 us (6%)
  other arithmetic  5.47 us (2%)
    pallas_call x1, Pallas kernels, gather_all(): pl.pallas_call(functools.partial(gather_kernel, count, plans, len(blocks)...  130 us
    pallas_call x1, Pallas kernels, scatter_all(): pl.pallas_call(functools.partial(scatter_kernel, count, plans, len(blocks...  124 us
    dot_general x4, matrix products, matmul_tn(): lax.dot_general(former, latter, (((0,), (0,)), ((), ())), preferred_eleme...  16.8 us
    dot_general x4, matrix products, matmul_nt(): lax.dot_general(former, latter, (((1,), (1,)), ((), ())), preferred_eleme...  14 us
    unnamed x58, local copies, waits for them, and re-layouts  9.68 us
    dot_general x4, matrix products, matmul(): return jnp.dot(former, latter, preferred_element_type=jnp.float32)  8.26 us

profile of v1, /device:TPU:0, one launch (start us, length us, event | category | flops | bytes accessed | tf_op | source)
XLA Modules:
  0.0 331.2 jit_solution(3903478233712125713)
XLA Ops:
  0.6 0.0 copy-start.6
  0.6 1.3 reshape.271.refs_4_
  1.9 0.8 broadcast_compare_fusion
  2.7 1.5 reshape.268.refs_1_
  4.3 1.7 reshape.267.refs_0_
  5.9 1.8 reshape.269.refs_2_
  7.7 1.8 reshape.270.refs_3_
  9.5 130.5 %shard_map.135 = (bf16[32,32,3072]{2,1,0:T(8,128)(2,1)}, bf16[32,32,1024]{2,1,0:T(8,128)(2,1)}, bf16[32,32,4096]{2,1,0:T(8,128)(2,1)}, bf16[32,128,1024]{2,1,0:T(8,128)(2,1)}, bf16[32,1,384]{2,1,0:T(2,128)(2,1)}) custom-call(bf16[32,3072]{1,0:T(8,128)(2,1)} %reshape.267.refs_0_, bf16[32,1024]{1,0:T(8,128)(2,1)} %reshape.268.refs_1_, ...), custom_call_target="tpu_custom_call" | custom-call | tf_op jit(solution)/shard_map/pallas_call | solution.py:470
  140.0 1.0 convert_element_type.110
  141.0 4.9 %convolution_bitcast_fusion = f32[128,3072]{0,1:T(8,128)S(1)} fusion(bf16[1024,3072]{1,0:T(8,128)(2,1)} %bitcast.79, bf16[128,1024]{1,0:T(8,128)(2,1)S(1)} %copy-done.6), kind=kOutput, calls=%fused_computation.6 | convolution fusion | flops 805306368 | bytes 8126464 | tf_op jit(solution)/shard_map/dot_general | solution.py:22
  145.9 0.3 fusion.26
  146.3 0.0 copy-start.8
  146.3 0.4 fusion.57
  146.7 0.2 exponential_reduce_fusion
  146.9 0.1 copy-done.14
  147.0 0.3 convolution_convert_fusion.6
  147.3 1.3 copy-done.1
  148.6 0.5 fusion.58
  149.1 0.2 multiply_reduce_fusion.4
  149.4 1.3 convolution_add_fusion
  150.7 0.6 slice-done.2
  151.3 1.3 slice-done.3
  152.7 1.5 fusion.59
  154.2 0.2 multiply_reduce_fusion.3
  154.4 0.3 fusion.25
  154.7 1.0 fusion.51
  155.7 3.4 %fusion.62 = (f32[4096]{0:T(1024)S(1)}, bf16[128,4096]{1,0:T(8,128)(2,1)S(1)}) fusion(f32[128,4096]{1,0:T(8,128)S(1)} %convolution_add_fusion, bf16[4096,1024]{1,0:T(8,128)(2,1)S(1)} %bitcast.78, f32[128,1024]{1,0:T(8,128)S(1)} %get-tuple-element.36), kind=kOutput, calls=%fused_computation.108 | convolution fusion | flops 1079635968 | bytes 12075008 | tf_op jit(solution)/shard_map/dot_general | solution.py:32
  159.1 3.0 multiply_reduce_fusion.1
  162.2 0.2 fusion.53
  162.4 1.5 convolution_convert_fusion.5
  163.9 1.1 copy.22
  165.1 2.4 fusion.54
  167.5 0.1 reduce_sum.188
  167.6 2.3 fusion.63
  169.9 3.6 %convolution_convert_fusion.4 = bf16[16,64,128]{2,1,0:T(8,128)(2,1)} fusion(bf16[128,16,64]{0,2,1:T(8,128)(2,1)} %bitcast.95, f32[16,128,128]{1,2,0:T(8,128)} %fusion.63, f32[16,128,128]{1,2,0:T(8,128)} %copy-done, f32[16,128]{1,0:T(8,128)S(1)} %log_add_fusion), kind=kOutput, calls=%fused_computation.30 | convolution fusion | flops 35522688 | bytes 2629632 | tf_op jit(solution)/shard_map/bhqk,bqhd->bkhd/dot_general | solution.py:125
  173.5 3.7 %fusion.55 = (f32[16,64]{1,0:T(8,128)S(1)}, bf16[1,128,16,64]{1,3,2,0:T(8,128)(2,1)}) fusion(bf16[128,16,64]{0,2,1:T(8,128)(2,1)} %bitcast.93, f32[16,128,128]{1,2,0:T(8,128)} %fusion.63, f32[16,128,128]{1,2,0:T(8,128)} %copy-done, f32[16,128]{1,0:T(8,128)S(1)} %log_add_fusion), kind=kOutput, calls=%fused_computation.103 | convolution fusion | flops 35652736 | bytes 2633728 | tf_op jit(solution)/shard_map/bhqk,bkhd->bqhd/dot_general | solution.py:122
  177.1 0.1 reduce_sum.186
  177.2 6.0 %fusion.12 = bf16[128,1024]{1,0:T(8,128)(2,1)} fusion(f32[128,1024]{1,0:T(8,128)} %copy-done.2, bf16[1024,3072]{1,0:T(8,128)(2,1)} %bitcast.80, bf16[128,1024]{0,1:T(8,128)(2,1)S(1)} %bitcast.90, bf16[128,1024]{0,1:T(8,128)(2,1)} %bitcast.102, bf16[128,1024]{0,1:T(8,128)(2,1)} %bitcast.104), kind=kOutput, calls=%fused_computation.29 | convolution fusion | flops 807927808 | bytes 7864320 | tf_op jit(solution)/shard_map/dot_general | solution.py:32
  183.3 2.0 convolution_convert_fusion.3
  185.4 4.5 %convolution_convert_fusion.2 = bf16[3072,1024]{0,1:T(8,128)(2,1)} fusion(bf16[128,1024]{1,0:T(8,128)(2,1)S(1)} %copy-done.7, bf16[128,1024]{0,1:T(8,128)(2,1)S(1)} %bitcast.91, bf16[128,1024]{0,1:T(8,128)(2,1)S(1)} %bitcast.103, bf16[128,1024]{0,1:T(8,128)(2,1)S(1)} %bitcast.105), kind=kOutput, calls=%fused_computation.3 | convolution fusion | flops 810811392 | bytes 7340032 | tf_op jit(solution)/shard_map/dot_general | solution.py:26
  189.9 4.6 %convolution_convert_fusion.1 = bf16[4096,1024]{1,0:T(8,128)(2,1)} fusion(f32[128,1024]{1,0:T(8,128)S(1)} %get-tuple-element.36, f32[128,4096]{1,0:T(8,128)S(1)} %convolution_add_fusion), kind=kOutput, calls=%fused_computation.2 | convolution fusion | flops 1080688640 | bytes 11010048 | tf_op jit(solution)/shard_map/dot_general | solution.py:26
  194.4 5.7 %convolution_convert_fusion = bf16[1024,4096]{1,0:T(8,128)(2,1)} fusion(bf16[128,4096]{1,0:T(8,128)(2,1)S(1)} %copy-done.5, f32[128,1024]{1,0:T(8,128)S(1)} %get-tuple-element.57, f32[1024]{0:T(1024)S(1)} %get-tuple-element.49, f32[1024]{0:T(1024)S(1)} %get-tuple-element.50, f32[128]{0:T(128)S(1)} %add_rsqrt_fusion.1, f32[128]{0:T(128)S(1)} %broadcast_multiply_fusion.5), kind=kOutput, calls=%fused_computation.1 | convolution fusion | flops 1078591488 | bytes 9970688 | tf_op jit(solution)/shard_map/dot_general | solution.py:26
  200.1 123.5 %shard_map.136 = (f32[128,1024]{1,0:T(8,128)}, f32[32,4096]{1,0:T(8,128)}, f32[32,3072]{1,0:T(8,128)}, f32[32,1024]{1,0:T(8,128)}, f32[1,384]{1,0:T(1,128)}) custom-call(bf16[32,128,1024]{2,1,0:T(8,128)(2,1)} %bitcast.68, bf16[32,32,4096]{2,1,0:T(8,128)(2,1)} %bitcast.74, bf16[32,32,3072]{2,1,0:T(8,128)(2,1)} %bitcast.73, bf16[32,32,1024]{2,1,0:T(8,128)(2,1)} %bitcast.83, ...), custom_call_target="tpu_custom_call" | custom-call | tf_op jit(solution)/shard_map/pallas_call | solution.py:366
  323.6 1.9 copy.30
  325.5 1.6 copy.31
  327.1 1.3 reduce.8
  328.4 1.9 copy.32
  330.3 0.9 copy.33
  (62 shorter events, 0.2 us)
Async XLA Ops:
  0.6 140.4 %copy-start.6 = (bf16[128,1024]{1,0:T(8,128)(2,1)S(1)}, bf16[128,1024]{1,0:T(8,128)(2,1)}, u32[]{:S(2)}) copy-start(bf16[128,1024]{1,0:T(8,128)(2,1)} %param.8) | copy-start | bytes 786436
  140.0 9.4 %slice-start = ((s8[8388608]{0:T(1024)(128)(4,1)}), s8[4194304]{0:T(1024)(128)(4,1)S(1)}, s32[]{:S(2)}) async-start(s8[8388608]{0:T(1024)(128)(4,1)} %bitcast.69), calls=%async_computation | async-start | bytes 8388608
  141.0 8.3 %slice-start.1 = ((s8[8388608]{0:T(1024)(128)(4,1)}), s8[4194304]{0:T(1024)(128)(4,1)S(1)}, s32[]{:S(2)}) async-start(s8[8388608]{0:T(1024)(128)(4,1)} %bitcast.69), calls=%async_computation.1 | async-start | bytes 8388608
  145.9 0.9 copy-start.13
  146.3 0.7 copy-start.14
  146.3 1.0 copy-start.8
  146.3 2.3 copy-start.1
  146.7 2.4 copy-start
  147.3 1.8 copy-start.9
  149.1 2.2 slice-start.2
  149.4 3.3 slice-start.3
  152.7 1.7 copy-start.11
  159.1 3.0 copy-start.4
  162.4 1.5 copy-start.2
  169.9 7.4 %copy-start.12 = (bf16[1,128,16,64]{1,3,2,0:T(8,128)(2,1)S(1)}, bf16[1,128,16,64]{1,3,2,0:T(8,128)(2,1)}, u32[]{:S(2)}) copy-start(bf16[1,128,16,64]{1,3,2,0:T(8,128)(2,1)} %get-tuple-element.43) | copy-start | bytes 786436
  177.2 6.1 %copy-start.3 = (f32[128,1024]{1,0:T(8,128)S(1)}, f32[128,1024]{1,0:T(8,128)}, u32[]{:S(2)}) copy-start(f32[128,1024]{1,0:T(8,128)} %copy-done.2) | copy-start | bytes 1572868
  177.2 6.1 %copy-start.10 = (bf16[16,64,128]{2,1,0:T(8,128)(2,1)S(1)}, bf16[16,64,128]{2,1,0:T(8,128)(2,1)}, u32[]{:S(2)}) copy-start(bf16[16,64,128]{2,1,0:T(8,128)(2,1)} %copy-done.9) | copy-start | bytes 786436
  183.2 2.2 copy-start.7
  183.2 2.2 copy-start.16
  183.2 2.2 copy-start.17
  183.3 6.6 %copy-start.18 = (f32[12288]{0:T(1024)}, f32[12288]{0:T(1024)S(1)}, u32[]{:S(2)}) copy-start(f32[12288]{0:T(1024)S(1)} %constant_dynamic-update-slice_fusion) | copy-start | bytes 147460
  189.9 4.6 %copy-start.5 = (bf16[128,4096]{1,0:T(8,128)(2,1)S(1)}, bf16[128,4096]{1,0:T(8,128)(2,1)}, u32[]{:S(2)}) copy-start(bf16[128,4096]{1,0:T(8,128)(2,1)} %copy-done.4) | copy-start | bytes 3145732
  323.6 6.7 %copy-start.15 = (f32[128,1024]{1,0:T(8,128)S(1)}, f32[128,1024]{1,0:T(8,128)}, u32[]{:S(2)}) copy-start(f32[128,1024]{1,0:T(8,128)} %get-tuple-element.25) | copy-start | bytes 1572868
